TPU v7x, 32 devices: a whole 2x2x4 slice. The times are simulated.
32 devices in a mesh: expert: 8 (over z, y), replica: 4 (over x, core).
Axes of the slice: x: 2, y: 2, z: 4, core: 2. Of those that a mesh axis runs over, the one named last changes fastest.
Arguments:
- tokens: bfloat16 [4096, 2048], P(('expert', 'replica')), may hold values from -6 to 6
- out_grad: bfloat16 [4096, 2048], P(('expert', 'replica')), may hold values from -6 to 6
- expert_ids: int32 [4096, 2], P(('expert', 'replica')), may hold values from 0 to 3, as said below
- route_weights: bfloat16 [4096, 2], P(('expert', 'replica')), may hold values from 0.25 to 1
- capacity: int32 [4], replicated, may hold values from 2 to 2
- w_gate: bfloat16 [8, 2048, 384], P('expert', 'replica'), may hold values from -0.125 to 0.125
- w_up: bfloat16 [8, 2048, 384], P('expert', 'replica'), may hold values from -0.125 to 0.125
- w_down: bfloat16 [8, 384, 2048], P('expert', None, 'replica'), may hold values from -0.21875 to 0.21875
Outputs:
- x_grad: bfloat16 [4096, 2048], P(('expert', 'replica'))
- gate_grad: bfloat16 [8, 2048, 384], P('expert', 'replica')
- up_grad: bfloat16 [8, 2048, 384], P('expert', 'replica')
- down_grad: bfloat16 [8, 384, 2048], P('expert')
Inputs may be any that keep to these rules, and one draw needn't show every extreme that they name: `expert_ids`: each row names 2 different experts.
All inputs are finite; a program needn't handle non-finite values.
Results may differ from a plain program's by a relative error of at most 0.009.
Values may be sent and summed in bfloat16 or wider, within the bound.
A program may use at most 64 MiB of HBM per device.

v0:
```python
import jax
import jax.numpy as jnp
from jax import lax
from jax.sharding import PartitionSpec as P

CAP = 2


def shards(tokens, out_grad, expert_ids, route_weights, capacity, w_gate, w_up, w_down):
    experts = capacity.shape[0]
    owners = lax.axis_size("expert")
    width = tokens.shape[1]
    slot_count = experts * CAP
    expert_range = jnp.arange(experts, dtype=jnp.int32)
    chosen = (expert_ids[:, :, None] == expert_range[None, None, :]).astype(jnp.int32)
    ranks = jnp.cumsum(jnp.sum(chosen, axis=1), axis=0)
    place = jnp.sum(chosen * ranks[:, None, :], axis=2) - 1
    limit = jnp.sum(chosen * capacity[None, None, :], axis=2)
    slot_ids = jnp.where(place < limit, expert_ids * CAP + place, -1)
    table = slot_ids[None, :, :] == jnp.arange(slot_count, dtype=jnp.int32)[:, None, None]
    picker = jnp.any(table, axis=2).astype(jnp.bfloat16)
    slot_weight = jnp.sum(
        jnp.where(table, route_weights.astype(jnp.float32)[None, :, :], 0.0), axis=(1, 2)
    ).astype(jnp.bfloat16)
    packed = jnp.dot(
        picker, jnp.concatenate([tokens, out_grad], axis=1), preferred_element_type=jnp.float32
    ).astype(jnp.bfloat16)
    packed = packed.reshape(experts, CAP, 2 * width)
    slot_weight = slot_weight.reshape(experts, CAP)
    send_rows = jnp.broadcast_to(packed[:, None], (experts, 2, CAP, 2 * width)).reshape(
        owners, CAP, 2 * width
    )
    send_weight = jnp.broadcast_to(slot_weight[:, None], (experts, 2, CAP)).reshape(owners, CAP)
    got_rows, got_weight = (
        lax.all_to_all(send_rows, "expert", split_axis=0, concat_axis=0, tiled=True),
        lax.all_to_all(send_weight, "expert", split_axis=0, concat_axis=0, tiled=True),
    )
    gate_all, up_all, down_all = (
        lax.all_gather(w_gate, "replica", axis=1, tiled=True),
        lax.all_gather(w_up, "replica", axis=1, tiled=True),
        lax.all_gather(w_down, "replica", axis=2, tiled=True),
    )
    gate_mat = gate_all[0]
    up_mat = up_all[0]
    down_mat = down_all[0]
    row_total = owners * CAP
    flat_rows = got_rows.reshape(row_total, 2 * width)
    inputs = flat_rows[:, :width]
    cotangent = flat_rows[:, width:]
    weights = got_weight.reshape(row_total).astype(jnp.float32)
    gate = jnp.dot(inputs, gate_mat, preferred_element_type=jnp.float32)
    up = jnp.dot(inputs, up_mat, preferred_element_type=jnp.float32)
    sig = jax.nn.sigmoid(gate)
    act = gate * sig
    hidden = (act * up).astype(jnp.bfloat16)
    scaled = (weights[:, None] * cotangent.astype(jnp.float32)).astype(jnp.bfloat16)
    back = lax.dot_general(
        scaled, down_mat, (((1,), (1,)), ((), ())), preferred_element_type=jnp.float32
    )
    gate_back = (back * up * sig * (1.0 + gate * (1.0 - sig))).astype(jnp.bfloat16)
    up_back = (back * act).astype(jnp.bfloat16)
    both_back = jnp.concatenate([gate_back, up_back], axis=1)
    both_mat = jnp.concatenate([gate_mat, up_mat], axis=1)
    partial_value = lax.dot_general(
        both_back, both_mat, (((1,), (1,)), ((), ())), preferred_element_type=jnp.float32
    ).astype(jnp.bfloat16)
    returned = lax.all_to_all(
        partial_value.reshape(owners, CAP, width), "expert", split_axis=0, concat_axis=0, tiled=True
    )
    returned = returned.reshape(experts, 2, CAP, width)
    total = lax.dot_general(
        picker,
        returned[:, 0].reshape(slot_count, width),
        (((0,), (0,)), ((), ())),
        preferred_element_type=jnp.float32,
    )
    total = total + lax.dot_general(
        picker,
        returned[:, 1].reshape(slot_count, width),
        (((0,), (0,)), ((), ())),
        preferred_element_type=jnp.float32,
    )
    x_grad = total.astype(jnp.bfloat16)
    wide_grad = lax.psum_scatter(
        lax.dot_general(
            inputs, both_back, (((0,), (0,)), ((), ())), preferred_element_type=jnp.float32
        )
        .astype(jnp.bfloat16)
        .astype(jnp.bfloat16),
        "replica",
        scatter_dimension=0,
        tiled=True,
    ).astype(jnp.float32)
    half_units = gate_mat.shape[1]
    gate_grad = wide_grad[:, :half_units].astype(jnp.bfloat16)[None]
    up_grad = wide_grad[:, half_units:].astype(jnp.bfloat16)[None]
    down_local = lax.dot_general(
        hidden, scaled, (((0,), (0,)), ((), ())), preferred_element_type=jnp.float32
    )
    down_grad = lax.psum(down_local.astype(jnp.bfloat16), "replica")[None]
    return (x_grad, gate_grad, up_grad, down_grad)


def solution(mesh):
    return jax.shard_map(
        shards,
        mesh=mesh,
        in_specs=(
            P(("expert", "replica"), None),
            P(("expert", "replica"), None),
            P(("expert", "replica"), None),
            P(("expert", "replica"), None),
            P(),
            P("expert", "replica", None),
            P("expert", "replica", None),
            P("expert", None, "replica"),
        ),
        out_specs=(
            P(("expert", "replica"), None),
            P("expert", "replica", None),
            P("expert", "replica", None),
            P("expert", None, None),
        ),
        check_vma=False,
    )
```

profile of v0, /device:TPU:0, one launch (start us, length us, event | category | flops | bytes accessed | tf_op | source)
XLA Modules:
  0.0 171.9 jit_solution(11029008983379027724)
XLA Ops:
  11.1 0.8 select_reduce_fusion.2
  13.7 7.3 %all-to-all-start = ((bf16[8,1,2]{2,1,0:T(2,128)(2,1)}), bf16[8,1,2]{2,1,0:T(2,128)(2,1)S(1)}, u32[]{:S(2)}, u32[]{:S(2)}) async-start(bf16[8,1,2]{2,1,0:T(2,128)(2,1)} %copy.30), calls=%async_computation | async-start | bytes 8192 | tf_op jit(solution)/shard_map/all_to_all | solution.py:36
  21.0 1.4 convolution_convert_fusion
  22.6 4.9 %all-to-all-done = bf16[8,1,2]{2,1,0:T(2,128)(2,1)S(1)} async-done(((bf16[8,1,2]{2,1,0:T(2,128)(2,1)}), bf16[8,1,2]{2,1,0:T(2,128)(2,1)S(1)}, u32[]{:S(2)}, u32[]{:S(2)}) %all-to-all-start) | async-done | bytes 64 | tf_op jit(solution)/shard_map/all_to_all | solution.py:36
  27.5 0.7 broadcast_in_dim.47
  28.2 3.4 %all-to-all-start.1 = ((bf16[8,2,4096]{2,1,0:T(2,128)(2,1)}), bf16[8,2,4096]{2,1,0:T(2,128)(2,1)S(1)}, u32[]{:S(2)}, u32[]{:S(2)}) async-start(bf16[8,2,4096]{2,1,0:T(2,128)(2,1)} %bitcast), calls=%async_computation.1 | async-start | bytes 262144 | tf_op jit(solution)/shard_map/all_to_all | solution.py:35
  31.7 7.1 %all-to-all-done.1 = bf16[8,2,4096]{2,1,0:T(2,128)(2,1)S(1)} async-done(((bf16[8,2,4096]{2,1,0:T(2,128)(2,1)}), bf16[8,2,4096]{2,1,0:T(2,128)(2,1)S(1)}, u32[]{:S(2)}, u32[]{:S(2)}) %all-to-all-start.1) | async-done | bytes 131104 | tf_op jit(solution)/shard_map/all_to_all | solution.py:35
  38.9 1.8 %fusion.17 = f32[16,384]{1,0:T(8,128)S(1)} fusion(bf16[16,4096]{1,0:T(8,128)(2,1)S(1)} %reshape.48, bf16[1,2048,384]{2,1,0:T(8,128)(2,1)} %all-gather.6.cloned.1.call-done), kind=kOutput, calls=%fused_computation.22 | convolution fusion | flops 25165824 | bytes 1662976 | tf_op jit(solution)/shard_map/dot_general | solution.py:52
  40.7 12.4 %all-gather.4.cloned.1.call-done = bf16[1,384,2048]{2,1,0:T(8,128)(2,1)} async-done(((bf16[1,384,512]{2,1,0:T(8,128)(2,1)}), bf16[1,384,2048]{2,1,0:T(8,128)(2,1)}) %all-gather.4.cloned.1.call-update) | async-done | bytes 1572880 | tf_op jit(solution)/shard_map/all_gather | solution.py:41
  53.1 1.9 %fusion.9 = f32[16,384]{1,0:T(8,128)S(1)} fusion(bf16[1,384,2048]{2,1,0:T(8,128)(2,1)} %all-gather.4.cloned.1.call-done, bf16[16,4096]{1,0:T(8,128)(2,1)S(1)} %reshape.48, f32[16]{0:T(128)S(1)} %reshape.51), kind=kOutput, calls=%fused_computation.11 | convolution fusion | flops 25264128 | bytes 1663488 | tf_op jit(solution)/shard_map/dot_general | solution.py:57
  55.1 19.3 %all-gather.8.cloned.1.call-done = bf16[1,2048,384]{2,1,0:T(8,128)(2,1)} async-done(((bf16[1,512,384]{2,1,0:T(8,128)(2,1)}), bf16[1,2048,384]{2,1,0:T(8,128)(2,1)}) %all-gather.8.cloned.1.call-update) | async-done | bytes 1572880 | tf_op jit(solution)/shard_map/all_gather | solution.py:39
  74.4 1.7 %multiply_convert_fusion.3 = (bf16[16,384]{1,0:T(8,128)(2,1)S(1)}, bf16[16,384]{1,0:T(8,128)(2,1)S(1)}, f32[16,384]{1,0:T(8,128)S(1)}) fusion(f32[16,384]{1,0:T(8,128)S(1)} %fusion.9, f32[16,384]{1,0:T(8,128)S(1)} %fusion.17, bf16[1,2048,384]{2,1,0:T(8,128)(2,1)} %all-gather.8.cloned.1.call-done, bf16[16,4096]{1,0:T(8,128)(2,1)S(1)} %reshape.48), kind=kOutput, calls=%fused_computation.27 | convolution fusion | flops 25245696 | bytes 1736704 | tf_op jit(solution)/shard_map/dot_general | solution.py:51
  76.1 2.7 %convolution_convert_fusion.1 = bf16[2048,768]{1,0:T(8,128)(2,1)} fusion(bf16[16,4096]{1,0:T(8,128)(2,1)S(1)} %reshape.48, bf16[16,384]{1,0:T(8,128)(2,1)S(1)} %get-tuple-element.11, bf16[16,384]{1,0:T(8,128)(2,1)S(1)} %get-tuple-element.10), kind=kOutput, calls=%fused_computation.1 | convolution fusion | flops 51953664 | bytes 3235840 | tf_op jit(solution)/shard_map/dot_general | solution.py:85
  78.8 1.4 copy-done
  80.7 0.9 fusion.6
  81.6 0.7 reshape.49
  82.3 5.5 %all-to-all-start.2 = ((bf16[8,2,2048]{2,1,0:T(2,128)(2,1)}), bf16[8,2,2048]{2,1,0:T(2,128)(2,1)S(1)}, u32[]{:S(2)}, u32[]{:S(2)}) async-start(bf16[8,2,2048]{2,1,0:T(2,128)(2,1)} %reshape.49), calls=%async_computation.2 | async-start | bytes 131072 | tf_op jit(solution)/shard_map/all_to_all | solution.py:67
  87.9 1.8 %fusion.4 = bf16[1,384,2048]{2,1,0:T(8,128)(2,1)} fusion(bf16[16,4096]{1,0:T(8,128)(2,1)S(1)} %reshape.48, f32[16]{0:T(128)S(1)} %reshape.51, f32[16,384]{1,0:T(8,128)S(1)} %fusion.17, f32[16,384]{1,0:T(8,128)S(1)} %get-tuple-element.12), kind=kOutput, calls=%fused_computation.7 | convolution fusion | flops 26087424 | bytes 1688064 | tf_op jit(solution)/shard_map/dot_general | solution.py:97
  89.7 5.1 %all-to-all-done.2 = bf16[8,2,2048]{2,1,0:T(2,128)(2,1)S(1)} async-done(((bf16[8,2,2048]{2,1,0:T(2,128)(2,1)}), bf16[8,2,2048]{2,1,0:T(2,128)(2,1)S(1)}, u32[]{:S(2)}, u32[]{:S(2)}) %all-to-all-start.2) | async-done | bytes 65568 | tf_op jit(solution)/shard_map/all_to_all | solution.py:67
  95.2 1.1 fusion.5
  96.3 20.6 %reduce-scatter.2.cloned.1.call-done = bf16[512,768]{1,0:T(8,128)(2,1)} async-done(((bf16[2048,768]{1,0:T(8,128)(2,1)}), bf16[512,768]{1,0:T(8,128)(2,1)}) %reduce-scatter.2.cloned.1.call-update) | async-done | bytes 786448 | tf_op jit(solution)/shard_map/reduce_scatter | solution.py:84
  116.9 2.1 %slice_bitcast_fusion = (bf16[1,512,384]{2,1,0:T(8,128)(2,1)}, bf16[1,512,384]{2,1,0:T(8,128)(2,1)}) fusion(bf16[512,768]{1,0:T(8,128)(2,1)} %reduce-scatter.2.cloned.1.call-done), kind=kLoop, calls=%fused_computation.16 | loop fusion | bytes 1572864 | tf_op jit(solution)/shard_map/broadcast_in_dim | solution.py:96
  119.0 43.6 %all-reduce.2.cloned.1.call-done = bf16[1,384,2048]{2,1,0:T(8,128)(2,1)} async-done(((bf16[1,384,2048]{2,1,0:T(8,128)(2,1)}), bf16[1,384,2048]{2,1,0:T(8,128)(2,1)}) %all-reduce.2.cloned.1.call-update) | async-done | bytes 1572880 | tf_op jit(solution)/shard_map/psum | solution.py:100
  162.6 2.7 %copy.32 = bf16[1,384,2048]{2,1,0:T(8,128)(2,1)} copy(bf16[1,384,2048]{2,1,0:T(8,128)(2,1)} %all-reduce.2.cloned.1.call-done) | data formatting | bytes 3145728
  (35 shorter events, 7.0 us)
Async XLA Ops:
  7.2 31.8 %all-gather.6.cloned.1.call-start = ((), (), s32[]{:S(2)}) async-start(), calls=%async_computation.5 | async-start | bytes 1966080 | tf_op jit(solution)/shard_map/all_gather | solution.py:40
  7.9 45.2 %all-gather.4.cloned.1.call-start = ((), (), s32[]{:S(2)}) async-start(), calls=%async_computation.4 | async-start | bytes 1966080 | tf_op jit(solution)/shard_map/all_gather | solution.py:41
  8.6 65.7 %all-gather.8.cloned.1.call-start = ((), (), s32[]{:S(2)}) async-start(), calls=%async_computation.6 | async-start | bytes 1966080 | tf_op jit(solution)/shard_map/all_gather | solution.py:39
  13.7 13.7 %all-to-all-start = ((bf16[8,1,2]{2,1,0:T(2,128)(2,1)}), bf16[8,1,2]{2,1,0:T(2,128)(2,1)S(1)}, u32[]{:S(2)}, u32[]{:S(2)}) async-start(bf16[8,1,2]{2,1,0:T(2,128)(2,1)} %copy.30), calls=%async_computation | async-start | bytes 8192 | tf_op jit(solution)/shard_map/all_to_all | solution.py:36
  28.2 10.7 %all-to-all-start.1 = ((bf16[8,2,4096]{2,1,0:T(2,128)(2,1)}), bf16[8,2,4096]{2,1,0:T(2,128)(2,1)S(1)}, u32[]{:S(2)}, u32[]{:S(2)}) async-start(bf16[8,2,4096]{2,1,0:T(2,128)(2,1)} %bitcast), calls=%async_computation.1 | async-start | bytes 262144 | tf_op jit(solution)/shard_map/all_to_all | solution.py:35
  31.6 85.4 %reduce-scatter.2.cloned.1.call-start = ((), (), s32[]{:S(2)}) async-start(), calls=%async_computation.7 | async-start | bytes 3932160 | tf_op jit(solution)/shard_map/reduce_scatter | solution.py:84
  78.8 1.4 copy-start
  78.8 1.9 %copy-start.1 = (bf16[1,2048,384]{2,1,0:T(8,128)(2,1)S(1)}, bf16[1,2048,384]{2,1,0:T(8,128)(2,1)}, u32[]{:S(2)}) copy-start(bf16[1,2048,384]{2,1,0:T(8,128)(2,1)} %all-gather.8.cloned.1.call-done) | copy-start | bytes 4718596
  82.3 12.4 %all-to-all-start.2 = ((bf16[8,2,2048]{2,1,0:T(2,128)(2,1)}), bf16[8,2,2048]{2,1,0:T(2,128)(2,1)S(1)}, u32[]{:S(2)}, u32[]{:S(2)}) async-start(bf16[8,2,2048]{2,1,0:T(2,128)(2,1)} %reshape.49), calls=%async_computation.2 | async-start | bytes 131072 | tf_op jit(solution)/shard_map/all_to_all | solution.py:67
  87.8 74.8 %all-reduce.2.cloned.1.call-start = ((), (), s32[]{:S(2)}) async-start(), calls=%async_computation.8 | async-start | bytes 3145728 | tf_op jit(solution)/shard_map/psum | solution.py:100
Sparse Core Ops, SparseCore 0:
  9.5 22.3 all-gather.5
  33.5 19.6 all-gather.3
  54.7 19.6 all-gather.7
  79.0 37.9 reduce-scatter.1
  119.7 42.8 all-reduce.1
where the time goes:
time: 172 us
  waiting for transfers between devices  115 us (67%)
  starting transfers between devices  16.4 us (10%)
  between operations  13.9 us (8%)
  matrix products  13.7 us (8%)
  local copies, waits for them, and re-layouts  9.59 us (6%)
  other arithmetic  3.13 us (2%)
    psum x1, waiting for transfers between devices, shards(): down_grad = lax.psum(down_local.astype(jnp.bfloat16), 'replica')[None]  43.6 us
    reduce_scatter x1, waiting for transfers between devices, shards(): lax.psum_scatter(lax.dot_general(inputs, both_back, (((0,), (0,)), ((), (...  20.6 us
    all_gather x1, waiting for transfers between devices, shards(): lax.all_gather(w_gate, 'replica', axis=1, tiled=True)  19.3 us
    all_gather x1, waiting for transfers between devices, shards(): lax.all_gather(w_down, 'replica', axis=2, tiled=True)  12.4 us
    all_to_all x1, starting transfers between devices, shards(): lax.all_to_all(send_weight, 'expert', split_axis=0, concat_axis=0, tiled=...  7.31 us
    all_to_all x1, waiting for transfers between devices, shards(): lax.all_to_all(send_rows, 'expert', split_axis=0, concat_axis=0, tiled=True)  7.13 us
    all_to_all x1, starting transfers between devices, shards(): lax.all_to_all(partial_value.reshape(owners, CAP, width), 'expert', split...  5.52 us
    all_to_all x1, waiting for transfers between devices, shards(): lax.all_to_all(partial_value.reshape(owners, CAP, width), 'expert', split...  5.08 us
  transfers between devices with their start and end apart: 8, of which 7 were waited for; matrix products, arithmetic and copies ran while one was open for 10% of the time, Pallas kernels for 0%

commit v1 on v0

v1 whole, which is shorter than its diff:
```python
import functools

import jax
import jax.numpy as jnp
from jax import lax
from jax.experimental import pallas as pl
from jax.experimental.pallas import tpu as pltpu
from jax.sharding import PartitionSpec as P

CAP = 2
F32, BF16 = jnp.float32, jnp.bfloat16


def dot(a, b, dims):
    return lax.dot_general(a, b, (dims, ((), ())), preferred_element_type=F32)


def kernel(
    n, reps, ids_ref, rw_ref, cap_ref, tok_ref, og_ref, wg_hbm, wu_hbm, wd_hbm,
    xg_ref, gg_ref, ug_ref, dg_ref,
    wg_ref, wu_ref, wd_ref, send, recv, cots, part, got1, got2, grads, rsend, rrecv,
    wsem, lsem, ssem, rsem,
):
    total = n * reps
    mo, mr = lax.axis_index("expert"), lax.axis_index("replica")
    me = mo * reps + mr
    core, pair = lax.rem(mr, 2), lax.div(mr, 2)
    block, width = tok_ref.shape
    dr = width // reps
    half = wg_ref.shape[1]
    slots = n * CAP
    rows = total * CAP

    def remote(src, dst, k, o, r):
        return pltpu.make_async_remote_copy(
            src_ref=src, dst_ref=dst, send_sem=ssem.at[k], recv_sem=rsem.at[k],
            device_id={"expert": o, "replica": r}, device_id_type=pl.DeviceIdType.MESH,
        )

    def where(k):
        g = lax.rem(me + k, total)
        return g, lax.div(g, reps), lax.rem(g, reps)

    loads = [
        pltpu.make_async_copy(src, dst, wsem.at[i])
        for i, (src, dst) in enumerate(((wg_hbm, wg_ref), (wu_hbm, wu_ref), (wd_hbm, wd_ref)))
    ]
    for load in loads:
        load.start()

    barrier = pltpu.get_barrier_semaphore()

    @pl.loop(1, total)
    def _(k):
        _, o, r = where(k)
        pl.semaphore_signal(
            barrier, inc=1, device_id={"expert": o, "replica": r},
            device_id_type=pl.DeviceIdType.MESH,
        )

    column = lax.broadcasted_iota(jnp.int32, (block, slots), 1)
    expert = column // (2 * CAP)
    place = column % CAP
    limit = jnp.zeros((block, slots), jnp.int32)
    for e in range(cap_ref.shape[0]):
        limit = jnp.where(expert == e, cap_ref[e], limit)
    named = jnp.zeros((block, slots), F32)
    weight = jnp.zeros((block, slots), F32)
    for k in range(ids_ref.shape[1]):
        hit = ids_ref[:, k : k + 1] == expert
        named = named + jnp.where(hit, 1.0, 0.0)
        weight = weight + jnp.where(hit, rw_ref[:, k : k + 1].astype(F32), 0.0)
    lower = jnp.where(
        lax.broadcasted_iota(jnp.int32, (block, block), 0)
        >= lax.broadcasted_iota(jnp.int32, (block, block), 1),
        1.0, 0.0,
    ).astype(BF16)
    ranks = dot(lower, named.astype(BF16), ((1,), (0,)))
    kept = (named > 0.0) & (ranks == (place + 1).astype(F32)) & (place < limit)
    picker = jnp.where(kept, 1.0, 0.0)
    slot_weight = dot(
        (picker * weight).astype(BF16), jnp.ones((block, 128), BF16), ((0,), (0,))
    )[:, :1]
    picker = picker.astype(BF16)
    for r in range(reps):
        cols = pl.ds(r * dr, dr)
        picked = dot(picker, tok_ref[:, cols], ((0,), (0,)))
        scaled = dot(picker, og_ref[:, cols], ((0,), (0,))) * slot_weight
        send[:, r, 0] = picked.reshape(n, CAP, dr).astype(BF16)
        send[:, r, 1] = scaled.reshape(n, CAP, dr).astype(BF16)

    pl.semaphore_wait(barrier, total - 1)

    own = pltpu.make_async_copy(send.at[mo, mr], recv.at[:, me], lsem.at[0])
    own.start()

    @pl.loop(1, total)
    def _(k):
        _, o, r = where(k)
        remote(send.at[o, r], recv.at[:, me], 0, o, r).start()

    for load in loads:
        load.wait()
    own.wait()
    arrived = recv.at[:, pl.ds(0, total - 1)]
    pltpu.make_async_copy(arrived, arrived, rsem.at[0]).wait()

    inputs = recv[0].astype(F32).reshape(rows, dr).astype(BF16)
    cot = recv[1].astype(F32).reshape(rows, dr).astype(BF16)
    wg, wu, wd = wg_ref[...], wu_ref[...], wd_ref[...]
    part[:, :, :half] = dot(inputs, wg, ((1,), (0,))).reshape(2, rows // 2, half)
    part[:, :, half : 2 * half] = dot(inputs, wu, ((1,), (0,))).reshape(2, rows // 2, half)
    part[:, :, 2 * half :] = dot(cot, wd, ((1,), (1,))).reshape(2, rows // 2, half)
    mate = lax.bitwise_xor(mr, 1)
    first = remote(part.at[1 - core], got1, 1, mo, mate)
    first.start()
    first.wait()

    got2[pair] = (part[core] + got1[...]).astype(BF16)
    pairs = reps // 2
    second = []
    for k in range(1, pairs):
        to = lax.rem(pair + k, pairs) * 2 + core
        second.append(remote(got2.at[pair], got2.at[pair], 1 + k, mo, to))
        second[-1].start()
    for copy in second:
        copy.wait()

    spread = []
    for k in range(1, reps):
        to = lax.rem(mr + k, reps)
        spread.append(remote(recv.at[1], cots.at[mr], 1 + pairs + k, mo, to))
        spread[-1].start()

    summed = got2[0].astype(F32)
    for k in range(1, pairs):
        summed = summed + got2[k].astype(F32)
    gate, up, back = summed[:, :half], summed[:, half : 2 * half], summed[:, 2 * half :]
    sig = jax.nn.sigmoid(gate)
    act = gate * sig
    grads[core, :, :half] = (back * up * sig * (1.0 + gate * (1.0 - sig))).astype(BF16)
    grads[core, :, half : 2 * half] = (back * act).astype(BF16)
    grads[core, :, 2 * half :] = (act * up).astype(BF16)
    third = remote(grads.at[core], grads.at[core], 1 + pairs, mo, mate)
    third.start()
    third.wait()

    both = grads[...].reshape(rows, 3 * half)
    gate_back, up_back, hidden = both[:, :half], both[:, half : 2 * half], both[:, 2 * half :]
    result = dot(gate_back, wg, ((1,), (1,))) + dot(up_back, wu, ((1,), (1,)))
    rsend[...] = result.reshape(total, CAP, dr).astype(BF16)

    back_own = pltpu.make_async_copy(rsend.at[me], rrecv.at[mo, mr], lsem.at[1])
    back_own.start()
    ret = 1 + pairs + reps

    @pl.loop(1, total)
    def _(k):
        g, o, r = where(k)
        remote(rsend.at[g], rrecv.at[mo, mr], ret, o, r).start()

    gg_ref[...] = dot(inputs, gate_back, ((0,), (0,))).astype(BF16)
    ug_ref[...] = dot(inputs, up_back, ((0,), (0,))).astype(BF16)
    for copy in spread:
        copy.wait()
    cots[mr] = recv[1]
    for r in range(reps):
        c = cots[r].astype(F32).reshape(rows, dr).astype(BF16)
        dg_ref[:, pl.ds(r * dr, dr)] = dot(hidden, c, ((0,), (0,))).astype(BF16)

    back_own.wait()
    returned = rsend.at[pl.ds(0, total - 1)]
    pltpu.make_async_copy(returned, returned, rsem.at[ret]).wait()
    for r in range(reps):
        rows_r = rrecv[:, r].astype(F32).reshape(slots, dr).astype(BF16)
        xg_ref[:, pl.ds(r * dr, dr)] = dot(picker, rows_r, ((1,), (0,))).astype(BF16)
    pltpu.make_async_copy(arrived, arrived, ssem.at[0]).wait()
    pltpu.make_async_copy(returned, returned, ssem.at[ret]).wait()


def shards(n, reps, tokens, out_grad, expert_ids, route_weights, capacity, w_gate, w_up, w_down):
    block, width = tokens.shape
    dr, half = w_gate.shape[1:]
    total = n * reps
    rows = total * CAP
    sems = 2 + reps // 2 + reps
    vmem = pl.BlockSpec(memory_space=pltpu.VMEM)
    hbm = pl.BlockSpec(memory_space=pl.ANY)
    x_grad, gate_grad, up_grad, down_grad = pl.pallas_call(
        functools.partial(kernel, n, reps),
        out_shape=(
            jax.ShapeDtypeStruct((block, width), BF16),
            jax.ShapeDtypeStruct((dr, half), BF16),
            jax.ShapeDtypeStruct((dr, half), BF16),
            jax.ShapeDtypeStruct((half, width), BF16),
        ),
        in_specs=[vmem, vmem, pl.BlockSpec(memory_space=pltpu.SMEM), vmem, vmem, hbm, hbm, hbm],
        out_specs=(vmem,) * 4,
        scratch_shapes=[
            pltpu.VMEM((dr, half), BF16),
            pltpu.VMEM((dr, half), BF16),
            pltpu.VMEM((half, dr), BF16),
            pltpu.VMEM((n, reps, 2, CAP, dr), BF16),
            pltpu.VMEM((2, total, CAP, dr), BF16),
            pltpu.VMEM((reps, total, CAP, dr), BF16),
            pltpu.VMEM((2, rows // 2, 3 * half), F32),
            pltpu.VMEM((rows // 2, 3 * half), F32),
            pltpu.VMEM((reps // 2, rows // 2, 3 * half), BF16),
            pltpu.VMEM((2, rows // 2, 3 * half), BF16),
            pltpu.VMEM((total, CAP, dr), BF16),
            pltpu.VMEM((n, reps, CAP, dr), BF16),
            pltpu.SemaphoreType.DMA((3,)),
            pltpu.SemaphoreType.DMA((2,)),
            pltpu.SemaphoreType.DMA((sems,)),
            pltpu.SemaphoreType.DMA((sems,)),
        ],
        compiler_params=pltpu.CompilerParams(collective_id=0, has_side_effects=True),
    )(
        expert_ids, route_weights, capacity, tokens, out_grad,
        w_gate.reshape(dr, half), w_up.reshape(dr, half), w_down.reshape(half, dr),
    )
    return x_grad, gate_grad[None], up_grad[None], down_grad[None]


def solution(mesh):
    return jax.shard_map(
        functools.partial(shards, mesh.shape["expert"], mesh.shape["replica"]),
        mesh=mesh,
        in_specs=(
            P(("expert", "replica"), None),
            P(("expert", "replica"), None),
            P(("expert", "replica"), None),
            P(("expert", "replica"), None),
            P(),
            P("expert", "replica", None),
            P("expert", "replica", None),
            P("expert", None, "replica"),
        ),
        out_specs=(
            P(("expert", "replica"), None),
            P("expert", "replica", None),
            P("expert", "replica", None),
            P("expert", None, None),
        ),
        check_vma=False,
    )
```

time: 172 us -> 37.2 us (0.22)
  waiting for transfers between devices: 115 us -> 0 us
  Pallas kernels: 0 us -> 26.8 us
  starting transfers between devices: 16.4 us -> 0 us
  matrix products: 13.7 us -> 0 us
  between operations: 13.9 us -> 0.65 us
  other arithmetic: 3.13 us -> 0 us
    psum x1 -> x0, waiting for transfers between devices: 43.6 us -> none  [shards(): down_grad = lax.psum(down_local.astype(jnp.bfloat16), 'replica')[None]]
    all_gather x3 -> x0, waiting for transfers between devices: 31.8 us -> none  [the longest x1 19.3 us: shards(): lax.all_gather(w_gate, 'replica', axis=1, tiled=True)]
    pallas_call x0 -> x1, Pallas kernels: none -> 26.8 us  [shards(): pl.pallas_call(functools.partial(kernel, n, reps), out_shape=(jax.ShapeDt...]
    reduce_scatter x1 -> x0, waiting for transfers between devices: 20.6 us -> none  [shards(): lax.psum_scatter(lax.dot_general(inputs, both_back, (((0,), (0,)), ((), (...]
    all_to_all x3 -> x0, waiting for transfers between devices: 17.1 us -> none  [the longest x1 7.13 us: shards(): lax.all_to_all(send_rows, 'expert', split_axis=0, concat_axis=0, tiled=True)]
    all_to_all x3 -> x0, starting transfers between devices: 16.2 us -> none  [the longest x1 7.31 us: shards(): lax.all_to_all(send_weight, 'expert', split_axis=0, concat_axis=0, tiled=...]
    dot_general x9 -> x0, matrix products: 13.7 us -> none  [the longest x1 2.69 us: shards(): lax.dot_general(inputs, both_back, (((0,), (0,)), ((), ())), preferred_el...]
    unnamed x5 -> x8, local copies, waits for them, and re-layouts: 4.58 us -> 9.5 us
  transfers between devices with their start and end apart: 8 -> 0, of which waited for: 7 -> 0; matrix products, arithmetic and copies ran while one was open for 10% -> 0% of each run, Pallas kernels for 0% -> 0%
where the time goes in v1:
time: 37.2 us; the launch traced here: 37 us
  Pallas kernels  26.8 us (72%)
  local copies, waits for them, and re-layouts  9.5 us (26%)
  between operations  0.65 us (2%)
    pallas_call x1, Pallas kernels, shards(): pl.pallas_call(functools.partial(kernel, n, reps), out_shape=(jax.ShapeDt...  26.8 us
    unnamed x8, local copies, waits for them, and re-layouts  9.5 us

profile of v1, /device:TPU:0, one launch (start us, length us, event | category | flops | bytes accessed | tf_op | source)
XLA Modules:
  0.0 37.0 jit_solution(18397734791200698251)
XLA Ops:
  0.6 1.4 %copy.13.rw_ref = bf16[128,2]{1,0:T(8,128)(2,1)} copy(bf16[128,2]{0,1:T(2,128)(2,1)} %param.11) | data formatting | bytes 1024 | tf_op args[3]
  2.0 1.4 %copy.12.ids_ref = s32[128,2]{1,0:T(8,128)} copy(s32[128,2]{0,1:T(2,128)} %param.10) | data formatting | bytes 2048 | tf_op args[2]
  3.4 26.8 %shard_map.111 = (bf16[128,2048]{1,0:T(8,128)(2,1)}, bf16[512,384]{1,0:T(8,128)(2,1)}, bf16[512,384]{1,0:T(8,128)(2,1)}, bf16[384,2048]{1,0:T(8,128)(2,1)}) custom-call(s32[128,2]{1,0:T(8,128)} %copy.12.ids_ref, bf16[128,2]{1,0:T(8,128)(2,1)} %copy.13.rw_ref, s32[4]{0:T(128)} %cap_ref.1, bf16[128,2048]{1,0:T(8,128)(2,1)} %tok_ref.1, ...), custom_call_target="tpu_custom_call" | custom-call | tf_op jit(solution)/shard_map/pallas_call | solution.py:189
  30.2 0.0 copy-start
  30.2 2.0 %copy.18 = bf16[128,2048]{1,0:T(8,128)(2,1)} copy(bf16[128,2048]{1,0:T(8,128)(2,1)} %get-tuple-element.16) | data formatting | bytes 1048576
  32.2 1.8 %copy.19 = bf16[1,512,384]{2,1,0:T(8,128)(2,1)} copy(bf16[1,512,384]{2,1,0:T(8,128)(2,1)} %bitcast.11) | data formatting | bytes 786432
  34.0 1.8 %copy.20 = bf16[1,512,384]{2,1,0:T(8,128)(2,1)} copy(bf16[1,512,384]{2,1,0:T(8,128)(2,1)} %bitcast.10) | data formatting | bytes 786432
  35.8 0.0 copy-done
  35.8 1.1 %copy.21 = bf16[1,384,2048]{2,1,0:T(8,128)(2,1)} copy(bf16[1,384,2048]{2,1,0:T(8,128)(2,1)S(1)} %bitcast.6) | data formatting | bytes 3145728
Async XLA Ops:
  30.2 5.6 %copy-start = (bf16[384,2048]{1,0:T(8,128)(2,1)S(1)}, bf16[384,2048]{1,0:T(8,128)(2,1)}, u32[]{:S(2)}) copy-start(bf16[384,2048]{1,0:T(8,128)(2,1)} %get-tuple-element.11) | copy-start | bytes 4718596

commit v2 on v1

--- a/solution.py
+++ b/solution.py
@@ -16,10 +16,10 @@
 
 
 def kernel(
-    n, reps, ids_ref, rw_ref, cap_ref, tok_ref, og_ref, wg_hbm, wu_hbm, wd_hbm,
-    xg_ref, gg_ref, ug_ref, dg_ref,
-    wg_ref, wu_ref, wd_ref, send, recv, cots, part, got1, got2, grads, rsend, rrecv,
-    wsem, lsem, ssem, rsem,
+    n, reps, ids_ref, rw_ref, cap_ref, tok_hbm, og_hbm, wg_hbm, wu_hbm, wd_hbm,
+    pick_ref, back_ref, gg_ref, ug_ref, dg_ref,
+    tok_ref, og_ref, wg_ref, wu_ref, wd_ref, send, recv, cots, part, got1, got2, grads,
+    rsend, rrecv, wsem, lsem, ssem, rsem,
 ):
     total = n * reps
     mo, mr = lax.axis_index("expert"), lax.axis_index("replica")
@@ -30,6 +30,7 @@
     half = wg_ref.shape[1]
     slots = n * CAP
     rows = total * CAP
+    pairs = reps // 2
 
     def remote(src, dst, k, o, r):
         return pltpu.make_async_remote_copy(
@@ -43,7 +44,10 @@
 
     loads = [
         pltpu.make_async_copy(src, dst, wsem.at[i])
-        for i, (src, dst) in enumerate(((wg_hbm, wg_ref), (wu_hbm, wu_ref), (wd_hbm, wd_ref)))
+        for i, (src, dst) in enumerate((
+            (tok_hbm, tok_ref), (og_hbm, og_ref),
+            (wg_hbm, wg_ref), (wu_hbm, wu_ref), (wd_hbm, wd_ref),
+        ))
     ]
     for load in loads:
         load.start()
@@ -58,34 +62,35 @@
             device_id_type=pl.DeviceIdType.MESH,
         )
 
-    column = lax.broadcasted_iota(jnp.int32, (block, slots), 1)
-    expert = column // (2 * CAP)
-    place = column % CAP
-    limit = jnp.zeros((block, slots), jnp.int32)
+    row = lax.broadcasted_iota(jnp.int32, (slots, block), 0)
+    expert = row // (2 * CAP)
+    place = row % CAP
+    limit = jnp.zeros((slots, block), jnp.int32)
     for e in range(cap_ref.shape[0]):
         limit = jnp.where(expert == e, cap_ref[e], limit)
-    named = jnp.zeros((block, slots), F32)
-    weight = jnp.zeros((block, slots), F32)
-    for k in range(ids_ref.shape[1]):
-        hit = ids_ref[:, k : k + 1] == expert
+    named = jnp.zeros((slots, block), F32)
+    weight = jnp.zeros((slots, block), F32)
+    for k in range(ids_ref.shape[0]):
+        hit = ids_ref[k : k + 1, :] == expert
         named = named + jnp.where(hit, 1.0, 0.0)
-        weight = weight + jnp.where(hit, rw_ref[:, k : k + 1].astype(F32), 0.0)
-    lower = jnp.where(
+        weight = weight + jnp.where(hit, rw_ref[k : k + 1, :].astype(F32), 0.0)
+    upper = jnp.where(
         lax.broadcasted_iota(jnp.int32, (block, block), 0)
-        >= lax.broadcasted_iota(jnp.int32, (block, block), 1),
+        <= lax.broadcasted_iota(jnp.int32, (block, block), 1),
         1.0, 0.0,
     ).astype(BF16)
-    ranks = dot(lower, named.astype(BF16), ((1,), (0,)))
+    ranks = dot(named.astype(BF16), upper, ((1,), (0,)))
     kept = (named > 0.0) & (ranks == (place + 1).astype(F32)) & (place < limit)
     picker = jnp.where(kept, 1.0, 0.0)
-    slot_weight = dot(
-        (picker * weight).astype(BF16), jnp.ones((block, 128), BF16), ((0,), (0,))
-    )[:, :1]
+    slot_weight = jnp.sum(picker * weight, axis=1, keepdims=True)
     picker = picker.astype(BF16)
+    pick_ref[...] = picker
+    loads[0].wait()
+    loads[1].wait()
     for r in range(reps):
         cols = pl.ds(r * dr, dr)
-        picked = dot(picker, tok_ref[:, cols], ((0,), (0,)))
-        scaled = dot(picker, og_ref[:, cols], ((0,), (0,))) * slot_weight
+        picked = dot(picker, tok_ref[:, cols], ((1,), (0,)))
+        scaled = dot(picker, og_ref[:, cols], ((1,), (0,))) * slot_weight
         send[:, r, 0] = picked.reshape(n, CAP, dr).astype(BF16)
         send[:, r, 1] = scaled.reshape(n, CAP, dr).astype(BF16)
 
@@ -99,11 +104,19 @@
         _, o, r = where(k)
         remote(send.at[o, r], recv.at[:, me], 0, o, r).start()
 
-    for load in loads:
+    for load in loads[2:]:
         load.wait()
     own.wait()
     arrived = recv.at[:, pl.ds(0, total - 1)]
     pltpu.make_async_copy(arrived, arrived, rsem.at[0]).wait()
+
+    mate = lax.bitwise_xor(mr, 1)
+    peers = [lax.rem(pair + k, pairs) * 2 + core for k in range(1, pairs)]
+    across = [
+        remote(recv.at[1], cots.at[mr], 2 + pairs + k, mo, to) for k, to in enumerate(peers)
+    ]
+    for copy in across:
+        copy.start()
 
     inputs = recv[0].astype(F32).reshape(rows, dr).astype(BF16)
     cot = recv[1].astype(F32).reshape(rows, dr).astype(BF16)
@@ -111,26 +124,16 @@
     part[:, :, :half] = dot(inputs, wg, ((1,), (0,))).reshape(2, rows // 2, half)
     part[:, :, half : 2 * half] = dot(inputs, wu, ((1,), (0,))).reshape(2, rows // 2, half)
     part[:, :, 2 * half :] = dot(cot, wd, ((1,), (1,))).reshape(2, rows // 2, half)
-    mate = lax.bitwise_xor(mr, 1)
     first = remote(part.at[1 - core], got1, 1, mo, mate)
     first.start()
     first.wait()
 
     got2[pair] = (part[core] + got1[...]).astype(BF16)
-    pairs = reps // 2
-    second = []
-    for k in range(1, pairs):
-        to = lax.rem(pair + k, pairs) * 2 + core
-        second.append(remote(got2.at[pair], got2.at[pair], 1 + k, mo, to))
-        second[-1].start()
+    second = [remote(got2.at[pair], got2.at[pair], 2 + k, mo, to) for k, to in enumerate(peers)]
+    for copy in second:
+        copy.start()
     for copy in second:
         copy.wait()
-
-    spread = []
-    for k in range(1, reps):
-        to = lax.rem(mr + k, reps)
-        spread.append(remote(recv.at[1], cots.at[mr], 1 + pairs + k, mo, to))
-        spread[-1].start()
 
     summed = got2[0].astype(F32)
     for k in range(1, pairs):
@@ -143,6 +146,15 @@
     grads[core, :, 2 * half :] = (act * up).astype(BF16)
     third = remote(grads.at[core], grads.at[core], 1 + pairs, mo, mate)
     third.start()
+
+    base = 2 + 2 * pairs
+    passed = [remote(recv.at[1], cots.at[mr], base, mo, mate)]
+    passed[0].start()
+    for k in range(1, pairs):
+        across[k - 1].wait()
+        came = lax.rem(pair + pairs - k, pairs) * 2 + core
+        passed.append(remote(cots.at[came], cots.at[came], base + k, mo, mate))
+        passed[-1].start()
     third.wait()
 
     both = grads[...].reshape(rows, 3 * half)
@@ -152,7 +164,7 @@
 
     back_own = pltpu.make_async_copy(rsend.at[me], rrecv.at[mo, mr], lsem.at[1])
     back_own.start()
-    ret = 1 + pairs + reps
+    ret = base + pairs
 
     @pl.loop(1, total)
     def _(k):
@@ -161,7 +173,7 @@
 
     gg_ref[...] = dot(inputs, gate_back, ((0,), (0,))).astype(BF16)
     ug_ref[...] = dot(inputs, up_back, ((0,), (0,))).astype(BF16)
-    for copy in spread:
+    for copy in passed:
         copy.wait()
     cots[mr] = recv[1]
     for r in range(reps):
@@ -172,10 +184,24 @@
     returned = rsend.at[pl.ds(0, total - 1)]
     pltpu.make_async_copy(returned, returned, rsem.at[ret]).wait()
     for r in range(reps):
-        rows_r = rrecv[:, r].astype(F32).reshape(slots, dr).astype(BF16)
-        xg_ref[:, pl.ds(r * dr, dr)] = dot(picker, rows_r, ((1,), (0,))).astype(BF16)
+        back_ref[:, pl.ds(r * dr, dr)] = rrecv[:, r].astype(F32).reshape(slots, dr).astype(BF16)
     pltpu.make_async_copy(arrived, arrived, ssem.at[0]).wait()
     pltpu.make_async_copy(returned, returned, ssem.at[ret]).wait()
+
+
+def finish(pick_ref, back_ref, gg_in, ug_in, dg_in, xg_out, gg_out, ug_out, dg_out, xg, sem):
+    copies = [
+        pltpu.make_async_copy(src, dst, sem.at[i])
+        for i, (src, dst) in enumerate(
+            ((dg_in, dg_out), (gg_in, gg_out), (ug_in, ug_out), (xg, xg_out))
+        )
+    ]
+    for copy in copies[:3]:
+        copy.start()
+    xg[...] = dot(pick_ref[...], back_ref[...], ((0,), (0,))).astype(BF16)
+    copies[3].start()
+    for copy in copies:
+        copy.wait()
 
 
 def shards(n, reps, tokens, out_grad, expert_ids, route_weights, capacity, w_gate, w_up, w_down):
@@ -183,20 +209,20 @@
     dr, half = w_gate.shape[1:]
     total = n * reps
     rows = total * CAP
-    sems = 2 + reps // 2 + reps
+    sems = 3 + 3 * (reps // 2)
     vmem = pl.BlockSpec(memory_space=pltpu.VMEM)
     hbm = pl.BlockSpec(memory_space=pl.ANY)
-    x_grad, gate_grad, up_grad, down_grad = pl.pallas_call(
+    shapes = ((block, width), (dr, half), (dr, half), (half, width))
+    partial = pl.pallas_call(
         functools.partial(kernel, n, reps),
-        out_shape=(
-            jax.ShapeDtypeStruct((block, width), BF16),
-            jax.ShapeDtypeStruct((dr, half), BF16),
-            jax.ShapeDtypeStruct((dr, half), BF16),
-            jax.ShapeDtypeStruct((half, width), BF16),
+        out_shape=tuple(
+            pltpu.VMEM(shape, BF16) for shape in ((n * CAP, block), (n * CAP, width), *shapes[1:])
         ),
-        in_specs=[vmem, vmem, pl.BlockSpec(memory_space=pltpu.SMEM), vmem, vmem, hbm, hbm, hbm],
-        out_specs=(vmem,) * 4,
+        in_specs=[vmem, vmem, pl.BlockSpec(memory_space=pltpu.SMEM)] + [hbm] * 5,
+        out_specs=(vmem,) * 5,
         scratch_shapes=[
+            pltpu.VMEM((block, width), BF16),
+            pltpu.VMEM((block, width), BF16),
             pltpu.VMEM((dr, half), BF16),
             pltpu.VMEM((dr, half), BF16),
             pltpu.VMEM((half, dr), BF16),
@@ -209,16 +235,23 @@
             pltpu.VMEM((2, rows // 2, 3 * half), BF16),
             pltpu.VMEM((total, CAP, dr), BF16),
             pltpu.VMEM((n, reps, CAP, dr), BF16),
-            pltpu.SemaphoreType.DMA((3,)),
+            pltpu.SemaphoreType.DMA((5,)),
             pltpu.SemaphoreType.DMA((2,)),
             pltpu.SemaphoreType.DMA((sems,)),
             pltpu.SemaphoreType.DMA((sems,)),
         ],
         compiler_params=pltpu.CompilerParams(collective_id=0, has_side_effects=True),
     )(
-        expert_ids, route_weights, capacity, tokens, out_grad,
+        expert_ids.T, route_weights.T, capacity, tokens, out_grad,
         w_gate.reshape(dr, half), w_up.reshape(dr, half), w_down.reshape(half, dr),
     )
+    x_grad, gate_grad, up_grad, down_grad = pl.pallas_call(
+        finish,
+        out_shape=tuple(jax.ShapeDtypeStruct(shape, BF16) for shape in shapes),
+        in_specs=[vmem] * 5,
+        out_specs=(hbm,) * 4,
+        scratch_shapes=[pltpu.VMEM((block, width), BF16), pltpu.SemaphoreType.DMA((4,))],
+    )(*(pltpu.with_memory_space_constraint(p, pltpu.VMEM) for p in partial))
     return x_grad, gate_grad[None], up_grad[None], down_grad[None]
 
 

time: 37.2 us -> 26.9 us (0.72)
  local copies, waits for them, and re-layouts: 9.5 us -> 0 us
  Pallas kernels: 26.8 us -> 26 us
    unnamed x8 -> x0, local copies, waits for them, and re-layouts: 9.5 us -> none
    pallas_call x1 -> x2, Pallas kernels: 26.8 us -> 26 us  [the longest x1 24.4 us: shards(): pl.pallas_call(functools.partial(kernel, n, reps), out_shape=tuple((pltpu...]
where the time goes in v2:
time: 26.9 us; the launch traced here: 26.7 us
  Pallas kernels  26 us (97%)
  between operations  0.64 us (2%)
    pallas_call x1, Pallas kernels, shards(): pl.pallas_call(functools.partial(kernel, n, reps), out_shape=tuple((pltpu...  24.4 us
    pallas_call x1, Pallas kernels, shards(): pl.pallas_call(finish, out_shape=tuple((jax.ShapeDtypeStruct(shape, BF16)...  1.61 us

profile of v2, /device:TPU:0, one launch (start us, length us, event | category | flops | bytes accessed | tf_op | source)
XLA Modules:
  0.0 26.7 jit_solution(13723140509381041264)
XLA Ops:
  0.6 24.4 %shard_map.111 = (bf16[16,128]{1,0:T(8,128)(2,1)S(1)}, bf16[16,2048]{1,0:T(8,128)(2,1)S(1)}, bf16[512,384]{1,0:T(8,128)(2,1)S(1)}, bf16[512,384]{1,0:T(8,128)(2,1)S(1)}, bf16[384,2048]{1,0:T(8,128)(2,1)S(1)}) custom-call(s32[2,128]{1,0:T(2,128)} %bitcast.11, bf16[2,128]{1,0:T(2,128)(2,1)} %bitcast.12, s32[4]{0:T(128)} %cap_ref.1, bf16[128,2048]{1,0:T(8,128)(2,1)} %tok_hbm.1, ...), custom_call_target="tpu_custom_call" | custom-call | tf_op jit(solution)/shard_map/pallas_call | solution.py:216
  25.1 1.6 %shard_map.112 = (bf16[128,2048]{1,0:T(8,128)(2,1)}, bf16[512,384]{1,0:T(8,128)(2,1)}, bf16[512,384]{1,0:T(8,128)(2,1)}, bf16[384,2048]{1,0:T(8,128)(2,1)}) custom-call(bf16[16,128]{1,0:T(8,128)(2,1)S(1)} %get-tuple-element.13.pick_ref, bf16[16,2048]{1,0:T(8,128)(2,1)S(1)} %get-tuple-element.14.back_ref, bf16[512,384]{1,0:T(8,128)(2,1)S(1)} %get-tuple-element.15.gg_in, ...), custom_call_target="tpu_custom_call" | custom-call | tf_op jit(solution)/shard_map/pallas_call | solution.py:248

commit v3 on v2

v3 whole, which is shorter than its diff:
```python
import functools

import jax
import jax.numpy as jnp
from jax import lax
from jax.experimental import pallas as pl
from jax.experimental.pallas import tpu as pltpu
from jax.sharding import PartitionSpec as P

CAP = 2
F32, BF16 = jnp.float32, jnp.bfloat16


def dot(a, b, dims):
    return lax.dot_general(a, b, (dims, ((), ())), preferred_element_type=F32)


def kernel(
    n, reps, ids_ref, rw_ref, cap_ref, tok_hbm, og_hbm, wg_hbm, wu_hbm, wd_hbm,
    pick_ref, back_ref, gg_ref, ug_ref, dg_ref,
    tok_ref, og_ref, wg_ref, wu_ref, wd_ref, send, recv, xs, cots, sums, grads,
    rsend, rrecv, wsem, lsem, ssem, rsem,
):
    pairs = reps // 2
    sources = n * pairs
    mo, mr = lax.axis_index("expert"), lax.axis_index("replica")
    core, pair = lax.rem(mr, 2), lax.div(mr, 2)
    mate = mr + 1 - 2 * core
    me = mo * pairs + pair
    block, width = tok_ref.shape
    dr, half = wg_hbm.shape
    slots = n * CAP
    rows = sources * CAP
    turn = [lax.rem(pair + k, pairs) for k in range(pairs)]

    def remote(src, dst, k, o, r):
        return pltpu.make_async_remote_copy(
            src_ref=src, dst_ref=dst, send_sem=ssem.at[k], recv_sem=rsem.at[k],
            device_id={"expert": o, "replica": r}, device_id_type=pl.DeviceIdType.MESH,
        )

    def everyone(act):
        @pl.loop(1, n)
        def _(k):
            o = lax.rem(mo + k, n)
            for p in turn:
                act(o, p)

        for p in turn[1:]:
            act(mo, p)

    barrier = pltpu.get_barrier_semaphore()

    def hail(o, r):
        pl.semaphore_signal(
            barrier, inc=1, device_id={"expert": o, "replica": r},
            device_id_type=pl.DeviceIdType.MESH,
        )

    everyone(lambda o, p: hail(o, 2 * p + core))
    hail(mo, mate)

    loads = [
        pltpu.make_async_copy(src, dst, wsem.at[i])
        for i, (src, dst) in enumerate((
            (tok_hbm, tok_ref), (og_hbm, og_ref),
            (wg_hbm, wg_ref.at[core]), (wu_hbm, wu_ref.at[core]), (wd_hbm, wd_ref.at[core]),
        ))
    ]
    for load in loads:
        load.start()

    row = lax.broadcasted_iota(jnp.int32, (slots, block), 0)
    expert = row // (2 * CAP)
    place = row % CAP
    limit = jnp.zeros((slots, block), jnp.int32)
    for e in range(cap_ref.shape[0]):
        limit = jnp.where(expert == e, cap_ref[e], limit)
    named = jnp.zeros((slots, block), F32)
    weight = jnp.zeros((slots, block), F32)
    for k in range(ids_ref.shape[0]):
        hit = ids_ref[k : k + 1, :] == expert
        named = named + jnp.where(hit, 1.0, 0.0)
        weight = weight + jnp.where(hit, rw_ref[k : k + 1, :].astype(F32), 0.0)
    upper = jnp.where(
        lax.broadcasted_iota(jnp.int32, (block, block), 0)
        <= lax.broadcasted_iota(jnp.int32, (block, block), 1),
        1.0, 0.0,
    ).astype(BF16)
    ranks = dot(named.astype(BF16), upper, ((1,), (0,)))
    kept = (named > 0.0) & (ranks == (place + 1).astype(F32)) & (place < limit)
    picker = jnp.where(kept, 1.0, 0.0)
    slot_weight = jnp.sum(picker * weight, axis=1, keepdims=True)
    picker = picker.astype(BF16)
    pick_ref[...] = picker
    loads[0].wait()
    loads[1].wait()
    for r in range(reps):
        cols = pl.ds(r * dr, dr)
        picked = dot(picker, tok_ref[:, cols], ((1,), (0,)))
        scaled = dot(picker, og_ref[:, cols], ((1,), (0,))) * slot_weight
        send[:, r // 2, 0, r % 2] = picked.reshape(n, CAP, dr).astype(BF16)
        send[:, r // 2, 1, r % 2] = scaled.reshape(n, CAP, dr).astype(BF16)

    pl.semaphore_wait(barrier, sources)

    own = pltpu.make_async_copy(send.at[mo, pair], recv.at[:, :, me], lsem.at[0])
    own.start()
    everyone(
        lambda o, p: remote(send.at[o, p], recv.at[:, :, me], 0, o, 2 * p + core).start()
    )

    lent = [
        remote(src, dst.at[core], 2 + i, mo, mate)
        for i, (src, dst) in enumerate(((wg_hbm, wg_ref), (wu_hbm, wu_ref), (wd_hbm, wd_ref)))
    ]
    for copy in lent:
        copy.start()
    for load in loads[2:]:
        load.wait()
    own.wait()
    arrived = recv.at[:, :, pl.ds(0, sources - 1)]
    pltpu.make_async_copy(arrived, arrived, rsem.at[0]).wait()

    used = 5
    across = []
    for k in range(1, pairs):
        across.append(remote(recv.at[1], cots.at[core, pair], used, mo, 2 * turn[k] + core))
        across[-1].start()
        used += 1

    def flat(value):
        return value.astype(F32).reshape(rows, dr).astype(BF16)

    x0, x1 = flat(recv[0, 0]), flat(recv[0, 1])
    c0, c1 = flat(recv[1, 0]), flat(recv[1, 1])
    for copy in lent:
        copy.wait()
    wg, wu, wd = [wg_ref[0], wg_ref[1]], [wu_ref[0], wu_ref[1]], [wd_ref[0], wd_ref[1]]
    crossing = []
    for i in range(3):
        if i < 2:
            w = (wg, wu)[i]
            value = dot(x0, w[0], ((1,), (0,))) + dot(x1, w[1], ((1,), (0,)))
        else:
            value = dot(c0, wd[0], ((1,), (1,))) + dot(c1, wd[1], ((1,), (1,)))
        sums[i, pair] = value.astype(BF16)
        for k in range(1, pairs):
            crossing.append(
                remote(sums.at[i, pair], sums.at[i, pair], used, mo, 2 * turn[k] + core)
            )
            crossing[-1].start()
            used += 1
    for copy in crossing:
        copy.wait()

    def total(i):
        value = sums[i, 0].astype(F32)
        for k in range(1, pairs):
            value = value + sums[i, k].astype(F32)
        return value

    gate, up, back = total(0), total(1), total(2)
    sig = jax.nn.sigmoid(gate)
    act = gate * sig
    gate_back = (back * up * sig * (1.0 + gate * (1.0 - sig))).astype(BF16)
    up_back = (back * act).astype(BF16)
    for s in range(2):
        result = dot(gate_back, wg[s], ((1,), (1,))) + dot(up_back, wu[s], ((1,), (1,)))
        rsend[:, s] = result.reshape(sources, CAP, dr).astype(BF16)
    back_own = pltpu.make_async_copy(rsend.at[me], rrecv.at[mo, pair], lsem.at[1])
    back_own.start()
    everyone(
        lambda o, p: remote(
            rsend.at[o * pairs + p], rrecv.at[mo, pair], 1, o, 2 * p + core
        ).start()
    )

    grads[0, core] = gate_back
    grads[1, core] = up_back
    grads[2, core] = (act * up).astype(BF16)
    swaps = [
        remote(recv.at[0, 1 - core], xs.at[core], used, mo, mate),
        remote(grads.at[:, core], grads.at[:, core], used + 1, mo, mate),
        remote(recv.at[1], cots.at[core, pair], used + 2, mo, mate),
    ]
    for copy in swaps:
        copy.start()
    used += 3
    xs[core] = recv[0, core]
    for k in range(1, pairs):
        across[k - 1].wait()
        came = lax.rem(pair + pairs - k, pairs)
        swaps.append(remote(cots.at[core, came], cots.at[core, came], used, mo, mate))
        swaps[-1].start()
        used += 1
    cots[core, pair] = recv[1]
    for copy in swaps:
        copy.wait()

    inputs = xs[...].astype(F32).reshape(2 * rows, dr).astype(BF16)
    gg_ref[...] = dot(inputs, grads[0].reshape(2 * rows, half), ((0,), (0,))).astype(BF16)
    ug_ref[...] = dot(inputs, grads[1].reshape(2 * rows, half), ((0,), (0,))).astype(BF16)
    hidden = grads[2].reshape(2 * rows, half)
    for r in range(reps):
        c = cots[:, r // 2, r % 2].astype(F32).reshape(2 * rows, dr).astype(BF16)
        dg_ref[:, pl.ds(r * dr, dr)] = dot(hidden, c, ((0,), (0,))).astype(BF16)

    back_own.wait()
    returned = rsend.at[pl.ds(0, sources - 1)]
    pltpu.make_async_copy(returned, returned, rsem.at[1]).wait()
    for r in range(reps):
        parts = rrecv[:, r // 2, r % 2].astype(F32).reshape(slots, dr).astype(BF16)
        back_ref[:, pl.ds(r * dr, dr)] = parts
    pltpu.make_async_copy(arrived, arrived, ssem.at[0]).wait()
    pltpu.make_async_copy(returned, returned, ssem.at[1]).wait()


def finish(pick_ref, back_ref, gg_in, ug_in, dg_in, xg_out, gg_out, ug_out, dg_out, xg, sem):
    copies = [
        pltpu.make_async_copy(src, dst, sem.at[i])
        for i, (src, dst) in enumerate(
            ((dg_in, dg_out), (gg_in, gg_out), (ug_in, ug_out), (xg, xg_out))
        )
    ]
    for copy in copies[:3]:
        copy.start()
    xg[...] = dot(pick_ref[...], back_ref[...], ((0,), (0,))).astype(BF16)
    copies[3].start()
    for copy in copies:
        copy.wait()


def shards(n, reps, tokens, out_grad, expert_ids, route_weights, capacity, w_gate, w_up, w_down):
    block, width = tokens.shape
    dr, half = w_gate.shape[1:]
    pairs = reps // 2
    sources = n * pairs
    rows = sources * CAP
    sems = 8 + 5 * (pairs - 1)
    vmem = pl.BlockSpec(memory_space=pltpu.VMEM)
    hbm = pl.BlockSpec(memory_space=pl.ANY)
    shapes = ((block, width), (dr, half), (dr, half), (half, width))
    partial = pl.pallas_call(
        functools.partial(kernel, n, reps),
        out_shape=tuple(
            pltpu.VMEM(shape, BF16) for shape in ((n * CAP, block), (n * CAP, width), *shapes[1:])
        ),
        in_specs=[vmem, vmem, pl.BlockSpec(memory_space=pltpu.SMEM)] + [hbm] * 5,
        out_specs=(vmem,) * 5,
        scratch_shapes=[
            pltpu.VMEM((block, width), BF16),
            pltpu.VMEM((block, width), BF16),
            pltpu.VMEM((2, dr, half), BF16),
            pltpu.VMEM((2, dr, half), BF16),
            pltpu.VMEM((2, half, dr), BF16),
            pltpu.VMEM((n, pairs, 2, 2, CAP, dr), BF16),
            pltpu.VMEM((2, 2, sources, CAP, dr), BF16),
            pltpu.VMEM((2, sources, CAP, dr), BF16),
            pltpu.VMEM((2, pairs, 2, sources, CAP, dr), BF16),
            pltpu.VMEM((3, pairs, rows, half), BF16),
            pltpu.VMEM((3, 2, rows, half), BF16),
            pltpu.VMEM((sources, 2, CAP, dr), BF16),
            pltpu.VMEM((n, pairs, 2, CAP, dr), BF16),
            pltpu.SemaphoreType.DMA((5,)),
            pltpu.SemaphoreType.DMA((2,)),
            pltpu.SemaphoreType.DMA((sems,)),
            pltpu.SemaphoreType.DMA((sems,)),
        ],
        compiler_params=pltpu.CompilerParams(collective_id=0, has_side_effects=True),
    )(
        expert_ids.T, route_weights.T, capacity, tokens, out_grad,
        w_gate.reshape(dr, half), w_up.reshape(dr, half), w_down.reshape(half, dr),
    )
    x_grad, gate_grad, up_grad, down_grad = pl.pallas_call(
        finish,
        out_shape=tuple(jax.ShapeDtypeStruct(shape, BF16) for shape in shapes),
        in_specs=[vmem] * 5,
        out_specs=(hbm,) * 4,
        scratch_shapes=[pltpu.VMEM((block, width), BF16), pltpu.SemaphoreType.DMA((4,))],
    )(*(pltpu.with_memory_space_constraint(p, pltpu.VMEM) for p in partial))
    return x_grad, gate_grad[None], up_grad[None], down_grad[None]


def solution(mesh):
    return jax.shard_map(
        functools.partial(shards, mesh.shape["expert"], mesh.shape["replica"]),
        mesh=mesh,
        in_specs=(
            P(("expert", "replica"), None),
            P(("expert", "replica"), None),
            P(("expert", "replica"), None),
            P(("expert", "replica"), None),
            P(),
            P("expert", "replica", None),
            P("expert", "replica", None),
            P("expert", None, "replica"),
        ),
        out_specs=(
            P(("expert", "replica"), None),
            P("expert", "replica", None),
            P("expert", "replica", None),
            P("expert", None, None),
        ),
        check_vma=False,
    )
```

time: 26.9 us -> 25 us (0.929)
  Pallas kernels: 26 us -> 24.2 us
    pallas_call x1, Pallas kernels: 24.4 us -> 22.6 us  [shards(): pl.pallas_call(functools.partial(kernel, n, reps), out_shape=tuple((pltpu...]
where the time goes in v3:
time: 25 us; the launch traced here: 24.8 us
  Pallas kernels  24.2 us (97%)
  between operations  0.64 us (3%)
    pallas_call x1, Pallas kernels, shards(): pl.pallas_call(functools.partial(kernel, n, reps), out_shape=tuple((pltpu...  22.6 us
    pallas_call x1, Pallas kernels, shards(): pl.pallas_call(finish, out_shape=tuple((jax.ShapeDtypeStruct(shape, BF16)...  1.61 us

profile of v3, /device:TPU:0, one launch (start us, length us, event | category | flops | bytes accessed | tf_op | source)
XLA Modules:
  0.0 24.8 jit_solution(3594606672353786949)
XLA Ops:
  0.6 22.6 %shard_map.111 = (bf16[16,128]{1,0:T(8,128)(2,1)S(1)}, bf16[16,2048]{1,0:T(8,128)(2,1)S(1)}, bf16[512,384]{1,0:T(8,128)(2,1)S(1)}, bf16[512,384]{1,0:T(8,128)(2,1)S(1)}, bf16[384,2048]{1,0:T(8,128)(2,1)S(1)}) custom-call(s32[2,128]{1,0:T(2,128)} %bitcast.11, bf16[2,128]{1,0:T(2,128)(2,1)} %bitcast.12, s32[4]{0:T(128)} %cap_ref.1, bf16[128,2048]{1,0:T(8,128)(2,1)} %tok_hbm.1, ...), custom_call_target="tpu_custom_call" | custom-call | tf_op jit(solution)/shard_map/pallas_call | solution.py:244
  23.2 1.6 %shard_map.112 = (bf16[128,2048]{1,0:T(8,128)(2,1)}, bf16[512,384]{1,0:T(8,128)(2,1)}, bf16[512,384]{1,0:T(8,128)(2,1)}, bf16[384,2048]{1,0:T(8,128)(2,1)}) custom-call(bf16[16,128]{1,0:T(8,128)(2,1)S(1)} %get-tuple-element.13.pick_ref, bf16[16,2048]{1,0:T(8,128)(2,1)S(1)} %get-tuple-element.14.back_ref, bf16[512,384]{1,0:T(8,128)(2,1)S(1)} %get-tuple-element.15.gg_in, ...), custom_call_target="tpu_custom_call" | custom-call | tf_op jit(solution)/shard_map/pallas_call | solution.py:275

commit v4 on v3

--- a/solution.py
+++ b/solution.py
@@ -42,7 +42,7 @@
     def everyone(act):
         @pl.loop(1, n)
         def _(k):
-            o = lax.rem(mo + k, n)
+            o = lax.rem(mo + lax.rem(k + n // 2 - 2 + n - 1, n - 1) + 1, n)
             for p in turn:
                 act(o, p)
 

time: 25 us -> 24.7 us (0.988)
  Pallas kernels: 24.2 us -> 23.9 us
    pallas_call x1, Pallas kernels: 22.6 us -> 22.3 us  [shards(): pl.pallas_call(functools.partial(kernel, n, reps), out_shape=tuple((pltpu...]
where the time goes in v4:
time: 24.7 us; the launch traced here: 24.6 us
  Pallas kernels  23.9 us (97%)
  between operations  0.64 us (3%)
    pallas_call x1, Pallas kernels, shards(): pl.pallas_call(functools.partial(kernel, n, reps), out_shape=tuple((pltpu...  22.3 us
    pallas_call x1, Pallas kernels, shards(): pl.pallas_call(finish, out_shape=tuple((jax.ShapeDtypeStruct(shape, BF16)...  1.61 us

profile of v4, /device:TPU:0, one launch (start us, length us, event | category | flops | bytes accessed | tf_op | source)
XLA Modules:
  0.0 24.6 jit_solution(15750282007742368476)
XLA Ops:
  0.6 22.3 %shard_map.111 = (bf16[16,128]{1,0:T(8,128)(2,1)S(1)}, bf16[16,2048]{1,0:T(8,128)(2,1)S(1)}, bf16[512,384]{1,0:T(8,128)(2,1)S(1)}, bf16[512,384]{1,0:T(8,128)(2,1)S(1)}, bf16[384,2048]{1,0:T(8,128)(2,1)S(1)}) custom-call(s32[2,128]{1,0:T(2,128)} %bitcast.11, bf16[2,128]{1,0:T(2,128)(2,1)} %bitcast.12, s32[4]{0:T(128)} %cap_ref.1, bf16[128,2048]{1,0:T(8,128)(2,1)} %tok_hbm.1, ...), custom_call_target="tpu_custom_call" | custom-call | tf_op jit(solution)/shard_map/pallas_call | solution.py:244
  22.9 1.6 %shard_map.112 = (bf16[128,2048]{1,0:T(8,128)(2,1)}, bf16[512,384]{1,0:T(8,128)(2,1)}, bf16[512,384]{1,0:T(8,128)(2,1)}, bf16[384,2048]{1,0:T(8,128)(2,1)}) custom-call(bf16[16,128]{1,0:T(8,128)(2,1)S(1)} %get-tuple-element.13.pick_ref, bf16[16,2048]{1,0:T(8,128)(2,1)S(1)} %get-tuple-element.14.back_ref, bf16[512,384]{1,0:T(8,128)(2,1)S(1)} %get-tuple-element.15.gg_in, ...), custom_call_target="tpu_custom_call" | custom-call | tf_op jit(solution)/shard_map/pallas_call | solution.py:275

commit v5 on v4

--- a/solution.py
+++ b/solution.py
@@ -42,7 +42,7 @@
     def everyone(act):
         @pl.loop(1, n)
         def _(k):
-            o = lax.rem(mo + lax.rem(k + n // 2 - 2 + n - 1, n - 1) + 1, n)
+            o = lax.rem(mo + lax.rem(k + n // 2 + 2 - 2 + n - 1, n - 1) + 1, n)
             for p in turn:
                 act(o, p)
 

time: 24.7 us -> 24.4 us (0.988)
  Pallas kernels: 23.9 us -> 23.5 us
    pallas_call x1, Pallas kernels: 22.3 us -> 21.9 us  [shards(): pl.pallas_call(functools.partial(kernel, n, reps), out_shape=tuple((pltpu...]
where the time goes in v5:
time: 24.4 us; the launch traced here: 24.2 us
  Pallas kernels  23.5 us (96%)
  between operations  0.64 us (3%)
    pallas_call x1, Pallas kernels, shards(): pl.pallas_call(functools.partial(kernel, n, reps), out_shape=tuple((pltpu...  21.9 us
    pallas_call x1, Pallas kernels, shards(): pl.pallas_call(finish, out_shape=tuple((jax.ShapeDtypeStruct(shape, BF16)...  1.61 us

profile of v5, /device:TPU:0, one launch (start us, length us, event | category | flops | bytes accessed | tf_op | source)
XLA Modules:
  0.0 24.2 jit_solution(10406977223701886537)
XLA Ops:
  0.6 21.9 %shard_map.111 = (bf16[16,128]{1,0:T(8,128)(2,1)S(1)}, bf16[16,2048]{1,0:T(8,128)(2,1)S(1)}, bf16[512,384]{1,0:T(8,128)(2,1)S(1)}, bf16[512,384]{1,0:T(8,128)(2,1)S(1)}, bf16[384,2048]{1,0:T(8,128)(2,1)S(1)}) custom-call(s32[2,128]{1,0:T(2,128)} %bitcast.11, bf16[2,128]{1,0:T(2,128)(2,1)} %bitcast.12, s32[4]{0:T(128)} %cap_ref.1, bf16[128,2048]{1,0:T(8,128)(2,1)} %tok_hbm.1, ...), custom_call_target="tpu_custom_call" | custom-call | tf_op jit(solution)/shard_map/pallas_call | solution.py:244
  22.6 1.6 %shard_map.112 = (bf16[128,2048]{1,0:T(8,128)(2,1)}, bf16[512,384]{1,0:T(8,128)(2,1)}, bf16[512,384]{1,0:T(8,128)(2,1)}, bf16[384,2048]{1,0:T(8,128)(2,1)}) custom-call(bf16[16,128]{1,0:T(8,128)(2,1)S(1)} %get-tuple-element.13.pick_ref, bf16[16,2048]{1,0:T(8,128)(2,1)S(1)} %get-tuple-element.14.back_ref, bf16[512,384]{1,0:T(8,128)(2,1)S(1)} %get-tuple-element.15.gg_in, ...), custom_call_target="tpu_custom_call" | custom-call | tf_op jit(solution)/shard_map/pallas_call | solution.py:275
